TPU v7x, 128 devices: a whole 4x4x4 slice. The times are simulated.
128 devices in a mesh: rows: 4 (over x_lo, core), hidden: 32 (over x_hi, z, y).
Axes of the slice: x: 4 (x_hi: 2, x_lo: 2; x = x_hi * 2 + x_lo), y: 4, z: 4, core: 2. Of those that a mesh axis runs over, the one named last changes fastest.
Arguments:
- resid_stream: bfloat16 [1024, 3584], P('rows'), may hold values from -6 to 6
- pre_gain: float32 [3584], replicated, may hold values from -0.5 to 0.5
- w_gate: bfloat16 [3584, 14336], P(None, 'hidden'), may hold values from -0.09375 to 0.09375
- w_up: bfloat16 [3584, 14336], P(None, 'hidden'), may hold values from -0.09375 to 0.09375
- w_down: bfloat16 [14336, 3584], P('hidden'), may hold values from -0.09375 to 0.09375
- w_enc: bfloat16 [3584, 32768], P(None, ('rows', 'hidden')), may hold values from -0.09375 to 0.09375
- b_enc: bfloat16 [32768], P(('rows', 'hidden')), may hold values from -3 to 3
- w_dec: bfloat16 [32768, 3584], P(('rows', 'hidden')), may hold values from -0.03125 to 0.03125
- b_dec: float32 [3584], replicated, may hold values from -3 to 3
Outputs:
- enc_grad: float32 [3584, 32768], P(None, ('rows', 'hidden'))
- dec_grad: float32 [32768, 3584], P(('rows', 'hidden'))
All inputs are finite; a program needn't handle non-finite values.
Results may differ from a plain program's by a relative error of at most 0.0062.
Values may be sent and summed in bfloat16 or wider, within the bound.
No kernel may reach another device: no remote copies, remote signals or barrier semaphores. Data moves between devices by JAX's collectives and lax.ppermute only.
A program may use at most 128 MiB of HBM per device.

v0:
```python
import math

import jax
import jax.numpy as jnp
from jax import lax
from jax.sharding import Mesh
from jax.sharding import PartitionSpec as P


F32 = jnp.float32
BF16 = jnp.bfloat16
ROWS = ("xl", "c")
HIDDEN = ("xh", "z", "y")
ALL = ("xl", "c", "xh", "z", "y")
SHIFTS = ((0, 0, 1), (1, 1, 0))


def scale_of(values):
    values = values.astype(F32)
    return lax.rsqrt(jnp.mean(values * values, axis=-1, keepdims=True) + 1e-06)


def normed(values, scale, gain):
    return (values.astype(F32) * scale * gain).astype(BF16)


def dot(left, right):
    return jnp.dot(left, right, preferred_element_type=F32)


def contract_first(left, right):
    return lax.dot_general(left, right, (((0,), (0,)), ((), ())), preferred_element_type=F32)


def contract_last(left, right):
    return lax.dot_general(left, right, (((1,), (1,)), ((), ())), preferred_element_type=F32)


def index_of(x, core, z, y):
    return (((x % 2) * 2 + core) * 2 + x // 2) * 16 + z * 4 + y


def devices():
    return [(x, core, z, y) for x in range(4) for core in range(2) for z in range(4) for y in range(4)]


def far_rows(values):
    pairs = [
        (index_of(x, core, z, y), index_of((x + 1 - 2 * core) % 4, core, z, y))
        for x, core, z, y in devices()
    ]
    return lax.ppermute(values, ALL, pairs)


def cube_groups(outer):
    groups = {}
    for x, core, z, y in devices():
        moved = [(v + step) % 4 for v, step in zip((x, z, y), SHIFTS[core])]
        cube = tuple(v // 2 for v in moved)
        place = tuple(min(v, 3 - v) for v in moved)
        key, order = (cube, place) if outer else (place, cube)
        groups.setdefault((core, key), []).append((order, index_of(x, core, z, y)))
    return [[device for _, device in sorted(members)] for _, members in sorted(groups.items())]


def exchange(values, outer):
    blocks = values.reshape(8, values.shape[0] // 8, values.shape[1])
    return lax.all_to_all(blocks, ALL, 0, 0, axis_index_groups=cube_groups(outer), tiled=True)


def spread(values, outer):
    copies = jnp.broadcast_to(values[None], (8,) + values.shape)
    got = lax.all_to_all(copies, ALL, 0, 0, axis_index_groups=cube_groups(outer), tiled=True)
    return got.reshape(8 * values.shape[0], values.shape[1])


def added(blocks):
    total = blocks[0].astype(F32)
    for block in blocks[1:]:
        total = total + block.astype(F32)
    return total


def other_core(values):
    return lax.ppermute(values, "c", [(0, 1), (1, 0)])


def paired(flag, first, second, blocks):
    rows, width = first.shape
    first, second = (v.reshape(blocks, 1, rows // blocks, width) for v in (first, second))
    forth = jnp.concatenate([first, second], axis=1)
    back = jnp.concatenate([second, first], axis=1)
    return jnp.where(flag, back, forth).reshape(2 * rows, width)


def on_device(resid_stream, pre_gain, w_gate, w_up, w_down, w_enc, b_enc, w_dec, b_dec):
    rows, _ = resid_stream.shape
    factor = 1.0 / math.sqrt(rows * lax.axis_size(ROWS))
    odd = lax.axis_index("xl") == 1

    far_resid = far_rows(resid_stream)
    enc_2 = jnp.concatenate([w_enc, other_core(w_enc)], axis=1)
    dec_2 = jnp.concatenate([w_dec, other_core(w_dec)], axis=0)
    bias_2 = jnp.concatenate([b_enc, other_core(b_enc)], axis=0).astype(F32)

    scale = scale_of(resid_stream)
    far_scale = far_rows(scale)
    near = normed(resid_stream, scale, 1.0 + pre_gain)
    hidden_units = (jax.nn.gelu(dot(near, w_gate), approximate=True) * dot(near, w_up)).astype(BF16)
    hidden_units = lax.optimization_barrier(hidden_units)
    near_act = jnp.maximum(dot(near, enc_2) + bias_2, 0.0)
    near_part = (
        dot((near_act * near_act).astype(BF16), dec_2) - dot(hidden_units, w_down)
    ).astype(BF16)
    far_resid, _ = lax.optimization_barrier((far_resid, near_part))
    got_near = exchange(near_part, True)
    gain = lax.optimization_barrier(pre_gain)
    gain = 1.0 + gain
    gain = lax.optimization_barrier(gain)
    far = normed(far_resid, far_scale, gain)
    far_act = jnp.maximum(dot(far, enc_2) + bias_2, 0.0)
    far_part = dot((far_act * far_act).astype(BF16), dec_2).astype(BF16)
    got_far = exchange(far_part, True)
    core = lax.axis_index("c")
    step = SHIFTS[0][0] + core * (SHIFTS[1][0] - SHIFTS[0][0])
    x = 2 * lax.axis_index("xh") + lax.axis_index("xl")
    turned = ((x + step) % 4 // 2 + step) % 2 == 1
    low = added(got_near[:4]) + added(got_far[4:])
    high = added(got_near[4:]) + added(got_far[:4])
    summed = paired(turned, low, high, 1).astype(BF16)
    misfit = (added(exchange(summed, False)) + b_dec).astype(BF16)
    misfit_all = spread(spread(misfit, False), True)

    rectified = paired(odd, near_act, far_act, 8)
    latent = (rectified * rectified).astype(BF16)

    own = w_dec.shape[0]
    dec_out = contract_first(latent[:, own:], misfit_all).astype(BF16)
    dec_sent = other_core(dec_out)
    misfit_all, dec_out = lax.optimization_barrier((misfit_all, dec_out))
    slope = (contract_last(misfit_all, dec_2) * 2.0 * rectified).astype(BF16)
    slope = slope.reshape(8, 2, -1, slope.shape[1])
    near_slope = jnp.where(odd, slope[:, 1], slope[:, 0]).reshape(rows, -1)
    far_slope = jnp.where(odd, slope[:, 0], slope[:, 1]).reshape(rows, -1)
    slope = jnp.concatenate([near_slope, far_slope], axis=0)
    normal_in = jnp.concatenate([near, far], axis=0)
    enc_out = contract_first(normal_in, slope[:, own:]).astype(BF16)
    enc_sent = other_core(enc_out)
    latent, slope, enc_out = lax.optimization_barrier((latent, slope, enc_out))
    dec_sum = (contract_first(latent[:, :own], misfit_all) + dec_sent.astype(F32)) * factor
    enc_sum = (contract_first(normal_in, slope[:, :own]) + enc_sent.astype(F32)) * factor
    return enc_sum, dec_sum


def solution(mesh):
    fine = Mesh(mesh.devices.reshape(2, 2, 2, 4, 4), ("xl", "c", "xh", "z", "y"))
    return jax.shard_map(
        on_device,
        mesh=fine,
        in_specs=(
            P(ROWS, None),
            P(),
            P(None, HIDDEN),
            P(None, HIDDEN),
            P(HIDDEN, None),
            P(None, ROWS + HIDDEN),
            P(ROWS + HIDDEN),
            P(ROWS + HIDDEN, None),
            P(),
        ),
        out_specs=(P(None, ROWS + HIDDEN), P(ROWS + HIDDEN, None)),
        check_vma=False,
    )
```

profile of v0, /device:TPU:1, one launch (start us, length us, event | category | flops | bytes accessed | tf_op | source)
XLA Modules:
  0.0 153.6 jit_solution(4315561165254168737)
XLA Ops:
  0.7 1.5 collective-permute-start.1
  2.6 2.6 %collective-permute-start = (bf16[256,3584]{1,0:T(8,128)(2,1)}, bf16[256,3584]{1,0:T(8,128)(2,1)S(1)}, u32[]{:S(2)}, u32[]{:S(2)}) collective-permute-start(bf16[256,3584]{1,0:T(8,128)(2,1)} %param.9), channel_id=1, source_target_pairs={{0,64},{1,65},{2,66},{3,67},{4,68},{5,69},{6,70},{7,71},{8,72},{9,... | collective-permute-start | bytes 5505032 | tf_op jit(solution)/shard_map/ppermute | solution.py:52
  5.2 2.0 %fusion.1 = f32[256]{0:T(256)S(1)} fusion(bf16[256,3584]{1,0:T(8,128)(2,1)} %param.9), kind=kLoop, calls=%fused_computation.7 | loop fusion | flops 2752256 | bytes 1836032 | tf_op jit(solution)/shard_map/reduce_sum | solution.py:20
  8.6 2.0 %fusion.3 = bf16[256,3584]{1,0:T(8,128)(2,1)S(1)} fusion(bf16[256,3584]{1,0:T(8,128)(2,1)} %param.9, f32[3584]{0:T(1024)S(1)} %broadcast_add_fusion.1, f32[256]{0:T(256)S(1)} %add_rsqrt_fusion), kind=kLoop, calls=%fused_computation.9 | loop fusion | flops 3670016 | bytes 3685376 | tf_op jit(solution)/shard_map/convert_element_type | solution.py:24
  11.7 1.5 copy-done.14
  14.9 1.2 fusion.31
  18.6 2.4 %fusion = bf16[256,3584]{1,0:T(8,128)(2,1)} fusion(f32[256,3584]{1,0:T(8,128)S(1)} %fusion.31, bf16[512,3584]{1,0:T(8,128)(2,1)S(1)} %constant_dynamic-update-slice_fusion.2, f32[256,512]{1,0:T(8,128)S(1)} %fusion.8), kind=kOutput, calls=%fused_computation.1 | convolution fusion | flops 941621248 | bytes 9699328 | tf_op jit(solution)/shard_map/dot_general | solution.py:28
  21.0 4.7 %collective-permute-done = bf16[256,3584]{1,0:T(8,128)(2,1)S(1)} collective-permute-done((bf16[256,3584]{1,0:T(8,128)(2,1)}, bf16[256,3584]{1,0:T(8,128)(2,1)S(1)}, u32[]{:S(2)}, u32[]{:S(2)}) %collective-permute-start) | collective-permute-done | bytes 1835040 | tf_op jit(solution)/shard_map/ppermute | solution.py:52
  27.4 1.1 convolution_convert_fusion.2
  28.5 21.1 %all_to_all.25 = bf16[8,32,3584]{2,1,0:T(8,128)(2,1)S(1)} all-to-all(bf16[8,32,3584]{2,1,0:T(8,128)(2,1)S(1)} %bitcast.38), channel_id=1, replica_groups={{3,0,7,4,67,64,71,68},{2,1,6,5,66,65,70,69},{15,12,11,8,79,76,75,72},{1..., dimensions={0} | all-to-all | bytes 3670016 | tf_op jit(solution)/shard_map/all_to_all | solution.py:68
  49.7 8.4 %all-to-all-start = ((bf16[8,32,3584]{2,1,0:T(8,128)(2,1)}), bf16[8,32,3584]{2,1,0:T(8,128)(2,1)}, u32[]{:S(2)}, u32[]{:S(2)}) async-start(bf16[8,32,3584]{2,1,0:T(8,128)(2,1)} %bitcast.5), calls=%async_computation | async-start | bytes 3670016 | tf_op jit(solution)/shard_map/all_to_all | solution.py:68
  58.1 12.2 %all-to-all-done = bf16[8,32,3584]{2,1,0:T(8,128)(2,1)} async-done(((bf16[8,32,3584]{2,1,0:T(8,128)(2,1)}), bf16[8,32,3584]{2,1,0:T(8,128)(2,1)}, u32[]{:S(2)}, u32[]{:S(2)}) %all-to-all-start) | async-done | bytes 1835040 | tf_op jit(solution)/shard_map/all_to_all | solution.py:68
  70.3 2.0 %add_bitcast_fusion.1 = (bf16[1,1,32,3584]{3,2,1,0:T(8,128)(2,1)S(1)}, bf16[1,1,32,3584]{3,2,1,0:T(8,128)(2,1)S(1)}) fusion(bf16[8,32,3584]{2,1,0:T(8,128)(2,1)S(1)} %all_to_all.25, bf16[8,32,3584]{2,1,0:T(8,128)(2,1)} %all-to-all-done), kind=kLoop, calls=%fused_computation.43 | loop fusion | flops 3670016 | bytes 4128768 | tf_op jit(solution)/shard_map/concatenate | solution.py:92
  72.4 11.6 %all_to_all.26 = bf16[8,8,3584]{2,1,0:T(8,128)(2,1)S(1)} all-to-all(bf16[8,8,3584]{2,1,0:T(8,128)(2,1)S(1)} %bitcast.42), channel_id=1, replica_groups={{3,2,15,14,83,82,95,94},{0,1,12,13,80,81,92,93},{7,6,11,10,87,86,91,90}..., dimensions={0} | all-to-all | bytes 917504 | tf_op jit(solution)/shard_map/all_to_all | solution.py:68
  84.1 10.2 %all_to_all.27 = bf16[8,8,3584]{2,1,0:T(8,128)(2,1)S(1)} all-to-all(bf16[8,8,3584]{2,1,0:T(8,128)(2,1)S(1)} %broadcast_in_dim.9), channel_id=1, replica_groups={{3,2,15,14,83,82,95,94},{0,1,12,13,80,81,92,93},{7,6,11,10,87,86,91,90}..., dimensions={0} | all-to-all | bytes 917504 | tf_op jit(solution)/shard_map/all_to_all | solution.py:73
  94.4 2.1 %broadcast_in_dim.11 = bf16[8,64,3584]{2,1,0:T(8,128)(2,1)} broadcast(bf16[64,3584]{1,0:T(8,128)(2,1)S(1)} %bitcast.43), dimensions={1,2} | broadcast | bytes 4128768 | tf_op jit(solution)/shard_map/broadcast_in_dim | solution.py:72
  96.5 8.4 %all-to-all-start.4 = ((bf16[8,64,3584]{2,1,0:T(8,128)(2,1)}), bf16[8,64,3584]{2,1,0:T(8,128)(2,1)}, u32[]{:S(2)}, u32[]{:S(2)}) async-start(bf16[8,64,3584]{2,1,0:T(8,128)(2,1)} %broadcast_in_dim.11), calls=%async_computation.4 | async-start | bytes 7340032 | tf_op jit(solution)/shard_map/all_to_all | solution.py:73
  105.2 22.6 %all-to-all-done.4 = bf16[8,64,3584]{2,1,0:T(8,128)(2,1)} async-done(((bf16[8,64,3584]{2,1,0:T(8,128)(2,1)}), bf16[8,64,3584]{2,1,0:T(8,128)(2,1)}, u32[]{:S(2)}, u32[]{:S(2)}) %all-to-all-start.4) | async-done | bytes 3670048 | tf_op jit(solution)/shard_map/all_to_all | solution.py:73
  127.7 3.3 %convolution_convert_fusion.1 = bf16[256,3584]{1,0:T(8,128)(2,1)S(1)} fusion(bf16[512,3584]{1,0:T(8,128)(2,1)} %bitcast.12, bf16[512,512]{1,0:T(8,128)(2,1)S(1)} %fusion.10), kind=kOutput, calls=%fused_computation.3 | convolution fusion | flops 940441600 | bytes 5767168 | tf_op jit(solution)/shard_map/dot_general | solution.py:32
  131.1 8.8 %collective-permute-start.6 = (bf16[256,3584]{1,0:T(8,128)(2,1)S(1)}, bf16[256,3584]{1,0:T(8,128)(2,1)S(1)}, u32[]{:S(2)}, u32[]{:S(2)}) collective-permute-start(bf16[256,3584]{1,0:T(8,128)(2,1)S(1)} %convolution_convert_fusion.1), channel_id=1, source_target_pairs={{0,32},{32,0},{1,33},{33,1},{2,34},{34,2},{3,35},{35,3},{4,36},{36... | collective-permute-start | bytes 5505032 | tf_op jit(solution)/shard_map/ppermute | solution.py:85
  139.9 4.3 %fusion.6 = bf16[512,512]{1,0:T(8,128)(2,1)S(1)} fusion(f32[512,512]{1,0:T(8,128)S(1)} %bitcast.39, bf16[512,3584]{1,0:T(8,128)(2,1)} %bitcast.12, bf16[512,3584]{1,0:T(8,128)(2,1)S(1)} %copy-done.3), kind=kOutput, calls=%fused_computation.17 | convolution fusion | flops 1879834624 | bytes 8912896 | tf_op jit(solution)/shard_map/dot_general | solution.py:36
  144.2 1.2 convolution_convert_fusion
  145.6 5.0 %add_multiply_fusion = f32[256,3584]{1,0:T(8,128)} fusion(bf16[256,3584]{1,0:T(8,128)(2,1)S(1)} %collective-permute-done.6, bf16[512,3584]{1,0:T(8,128)(2,1)} %bitcast.12, bf16[512,512]{1,0:T(8,128)(2,1)S(1)} %fusion.10), kind=kOutput, calls=%fused_computation.11 | convolution fusion | flops 942276608 | bytes 9437184 | tf_op jit(solution)/shard_map/dot_general | solution.py:32
  150.6 3.0 %add_multiply_fusion.1 = f32[3584,256]{1,0:T(8,128)} fusion(bf16[3584,256]{1,0:T(8,128)(2,1)S(1)} %collective-permute-done.5, bf16[256,3584]{1,0:T(8,128)(2,1)S(1)} %copy-done.9, bf16[256,3584]{1,0:T(8,128)(2,1)S(1)} %copy-done.7, bf16[512,512]{1,0:T(8,128)(2,1)S(1)} %pad_maximum_fusion.5), kind=kOutput, calls=%fused_computation.12 | convolution fusion | flops 949616640 | bytes 9437184 | tf_op jit(solution)/shard_map/dot_general | solution.py:32
  (60 shorter events, 9.3 us)
Async XLA Ops:
  0.6 14.2 %copy-start = (bf16[448,3584]{1,0:T(8,128)(2,1)S(1)}, bf16[448,3584]{1,0:T(8,128)(2,1)}, u32[]{:S(2)}) copy-start(bf16[448,3584]{1,0:T(8,128)(2,1)} %param.13) | copy-start | bytes 9633796
  0.6 10.0 %copy-start.13 = (bf16[3584,448]{0,1:T(8,128)(2,1)S(1)}, bf16[3584,448]{0,1:T(8,128)(2,1)}, u32[]{:S(2)}) copy-start(bf16[3584,448]{0,1:T(8,128)(2,1)} %param.11) | copy-start | bytes 9633796
  0.7 16.5 %collective-permute-start.1 = (bf16[3584,256]{1,0:T(8,128)(2,1)}, bf16[3584,256]{1,0:T(8,128)(2,1)S(1)}, u32[]{:S(2)}, u32[]{:S(2)}) collective-permute-start(bf16[3584,256]{1,0:T(8,128)(2,1)} %param.14), channel_id=1, source_target_pairs={{0,32},{32,0},{1,33},{33,1},{2,34},{34,2},{3,35},{35,3},{4,36},{36... | collective-permute-start | bytes 5505032 | tf_op jit(solution)/shard_map/ppermute | solution.py:85
  2.1 15.0 %collective-permute-start.2 = (bf16[256]{0:T(256)(128)(2,1)}, bf16[256]{0:T(256)(128)(2,1)S(1)}, u32[]{:S(2)}, u32[]{:S(2)}) collective-permute-start(bf16[256]{0:T(256)(128)(2,1)} %param.15), channel_id=1, source_target_pairs={{0,32},{32,0},{1,33},{33,1},{2,34},{34,2},{3,35},{35,3},{4,36},{36... | collective-permute-start | bytes 1544 | tf_op jit(solution)/shard_map/ppermute | solution.py:85
  2.2 16.2 %collective-permute-start.3 = (bf16[256,3584]{1,0:T(8,128)(2,1)}, bf16[256,3584]{1,0:T(8,128)(2,1)S(1)}, u32[]{:S(2)}, u32[]{:S(2)}) collective-permute-start(bf16[256,3584]{1,0:T(8,128)(2,1)} %param.16), channel_id=1, source_target_pairs={{0,32},{32,0},{1,33},{33,1},{2,34},{34,2},{3,35},{35,3},{4,36},{36... | collective-permute-start | bytes 5505032 | tf_op jit(solution)/shard_map/ppermute | solution.py:85
  2.6 23.1 %collective-permute-start = (bf16[256,3584]{1,0:T(8,128)(2,1)}, bf16[256,3584]{1,0:T(8,128)(2,1)S(1)}, u32[]{:S(2)}, u32[]{:S(2)}) collective-permute-start(bf16[256,3584]{1,0:T(8,128)(2,1)} %param.9), channel_id=1, source_target_pairs={{0,64},{1,65},{2,66},{3,67},{4,68},{5,69},{6,70},{7,71},{8,72},{9,... | collective-permute-start | bytes 5505032 | tf_op jit(solution)/shard_map/ppermute | solution.py:52
  7.2 18.5 %collective-permute-start.4 = (f32[256,1]{0,1:T(1,128)S(1)}, f32[256,1]{0,1:T(1,128)S(1)}, u32[]{:S(2)}, u32[]{:S(2)}) collective-permute-start(f32[256,1]{0,1:T(1,128)S(1)} %bitcast.49), channel_id=1, source_target_pairs={{0,64},{1,65},{2,66},{3,67},{4,68},{5,69},{6,70},{7,71},{8,72},{9,... | collective-permute-start | bytes 3080 | tf_op jit(solution)/shard_map/ppermute | solution.py:52
  10.6 6.7 %copy-start.6 = (bf16[256,3584]{1,0:T(8,128)(2,1)}, bf16[256,3584]{1,0:T(8,128)(2,1)S(1)}, u32[]{:S(2)}) copy-start(bf16[256,3584]{1,0:T(8,128)(2,1)S(1)} %fusion.3) | copy-start | bytes 5505028
  10.6 2.6 %copy-start.14 = (bf16[3584,448]{0,1:T(8,128)(2,1)S(1)}, bf16[3584,448]{0,1:T(8,128)(2,1)}, u32[]{:S(2)}) copy-start(bf16[3584,448]{0,1:T(8,128)(2,1)} %param.12) | copy-start | bytes 9633796
  13.2 1.5 copy-start.4
  14.9 1.5 copy-start.5
  16.4 0.7 copy-start.10
  16.4 0.7 copy-start.12
  18.5 8.8 %copy-start.2 = (bf16[512,3584]{1,0:T(8,128)(2,1)}, bf16[512,3584]{1,0:T(8,128)(2,1)S(1)}, u32[]{:S(2)}) copy-start(bf16[512,3584]{1,0:T(8,128)(2,1)S(1)} %constant_dynamic-update-slice_fusion.2) | copy-start | bytes 11010052
  26.2 2.3 %copy-start.8 = (bf16[256,3584]{1,0:T(8,128)(2,1)}, bf16[256,3584]{1,0:T(8,128)(2,1)S(1)}, u32[]{:S(2)}) copy-start(bf16[256,3584]{1,0:T(8,128)(2,1)S(1)} %multiply_convert_fusion) | copy-start | bytes 5505028
  49.7 20.6 %all-to-all-start = ((bf16[8,32,3584]{2,1,0:T(8,128)(2,1)}), bf16[8,32,3584]{2,1,0:T(8,128)(2,1)}, u32[]{:S(2)}, u32[]{:S(2)}) async-start(bf16[8,32,3584]{2,1,0:T(8,128)(2,1)} %bitcast.5), calls=%async_computation | async-start | bytes 3670016 | tf_op jit(solution)/shard_map/all_to_all | solution.py:68
  58.1 26.0 %copy-start.11 = (f32[3584]{0:T(1024)S(1)}, f32[3584]{0:T(1024)}, u32[]{:S(2)}) copy-start(f32[3584]{0:T(1024)} %param.17) | copy-start | bytes 43012
  96.5 31.2 %all-to-all-start.4 = ((bf16[8,64,3584]{2,1,0:T(8,128)(2,1)}), bf16[8,64,3584]{2,1,0:T(8,128)(2,1)}, u32[]{:S(2)}, u32[]{:S(2)}) async-start(bf16[8,64,3584]{2,1,0:T(8,128)(2,1)} %broadcast_in_dim.11), calls=%async_computation.4 | async-start | bytes 7340032 | tf_op jit(solution)/shard_map/all_to_all | solution.py:73
  127.7 12.2 %copy-start.3 = (bf16[512,3584]{1,0:T(8,128)(2,1)S(1)}, bf16[512,3584]{1,0:T(8,128)(2,1)}, u32[]{:S(2)}) copy-start(bf16[512,3584]{1,0:T(8,128)(2,1)} %copy-done.2) | copy-start | bytes 11010052
  131.1 14.5 %collective-permute-start.6 = (bf16[256,3584]{1,0:T(8,128)(2,1)S(1)}, bf16[256,3584]{1,0:T(8,128)(2,1)S(1)}, u32[]{:S(2)}, u32[]{:S(2)}) collective-permute-start(bf16[256,3584]{1,0:T(8,128)(2,1)S(1)} %convolution_convert_fusion.1), channel_id=1, source_target_pairs={{0,32},{32,0},{1,33},{33,1},{2,34},{34,2},{3,35},{35,3},{4,36},{36... | collective-permute-start | bytes 5505032 | tf_op jit(solution)/shard_map/ppermute | solution.py:85
  139.9 4.3 %copy-start.7 = (bf16[256,3584]{1,0:T(8,128)(2,1)S(1)}, bf16[256,3584]{1,0:T(8,128)(2,1)}, u32[]{:S(2)}) copy-start(bf16[256,3584]{1,0:T(8,128)(2,1)} %copy-done.6) | copy-start | bytes 5505028
  139.9 4.3 %copy-start.9 = (bf16[256,3584]{1,0:T(8,128)(2,1)S(1)}, bf16[256,3584]{1,0:T(8,128)(2,1)}, u32[]{:S(2)}) copy-start(bf16[256,3584]{1,0:T(8,128)(2,1)} %copy-done.8) | copy-start | bytes 5505028
  145.4 5.2 %collective-permute-start.5 = (bf16[3584,256]{1,0:T(8,128)(2,1)S(1)}, bf16[3584,256]{1,0:T(8,128)(2,1)S(1)}, u32[]{:S(2)}, u32[]{:S(2)}) collective-permute-start(bf16[3584,256]{1,0:T(8,128)(2,1)S(1)} %convolution_convert_fusion), channel_id=1, source_target_pairs={{0,32},{32,0},{1,33},{33,1},{2,34},{34,2},{3,35},{35,3},{4,36},{36... | collective-permute-start | bytes 5505032 | tf_op jit(solution)/shard_map/ppermute | solution.py:85
  150.6 3.0 %copy-start.1 = (bf16[448,3584]{1,0:T(8,128)(2,1)S(1)}, bf16[448,3584]{1,0:T(8,128)(2,1)}, u32[]{:S(2)}) copy-start(bf16[448,3584]{1,0:T(8,128)(2,1)} %param.13) | copy-start | bytes 9633796
where the time goes:
time: 154 us
  blocking collectives  43 us (28%)
  waiting for transfers between devices  39.5 us (26%)
  starting transfers between devices  31 us (20%)
  matrix products  25.8 us (17%)
  other arithmetic  7.64 us (5%)
  local copies, waits for them, and re-layouts  5.76 us (4%)
    all_to_all x2, blocking collectives, exchange(): lax.all_to_all(blocks, ALL, 0, 0, axis_index_groups=cube_groups(outer), t...  32.8 us
    all_to_all x1, waiting for transfers between devices, spread(): lax.all_to_all(copies, ALL, 0, 0, axis_index_groups=cube_groups(outer), t...  22.6 us
    dot_general x4, matrix products, contract_first(): lax.dot_general(left, right, (((0,), (0,)), ((), ())), preferred_element_...  12.5 us
    all_to_all x1, waiting for transfers between devices, exchange(): lax.all_to_all(blocks, ALL, 0, 0, axis_index_groups=cube_groups(outer), t...  12.2 us
    ppermute x5, starting transfers between devices, other_core(): return lax.ppermute(values, 'c', [(0, 1), (1, 0)])  10.9 us
    all_to_all x1, blocking collectives, spread(): lax.all_to_all(copies, ALL, 0, 0, axis_index_groups=cube_groups(outer), t...  10.2 us
    dot_general x7, matrix products, dot(): return jnp.dot(left, right, preferred_element_type=F32)  8.98 us
    all_to_all x1, starting transfers between devices, exchange(): lax.all_to_all(blocks, ALL, 0, 0, axis_index_groups=cube_groups(outer), t...  8.4 us
  transfers between devices with their start and end apart: 9, of which 3 were waited for; matrix products, arithmetic and copies ran while one was open for 15% of the time, Pallas kernels for 0%

commit v1 on v0

--- a/solution.py
+++ b/solution.py
@@ -12,7 +12,7 @@
 ROWS = ("xl", "c")
 HIDDEN = ("xh", "z", "y")
 ALL = ("xl", "c", "xh", "z", "y")
-SHIFTS = ((0, 0, 1), (1, 1, 0))
+LINE = 4
 
 
 def scale_of(values):
@@ -52,26 +52,28 @@
     return lax.ppermute(values, ALL, pairs)
 
 
-def cube_groups(outer):
+def groups_of(line):
     groups = {}
     for x, core, z, y in devices():
-        moved = [(v + step) % 4 for v, step in zip((x, z, y), SHIFTS[core])]
-        cube = tuple(v // 2 for v in moved)
-        place = tuple(min(v, 3 - v) for v in moved)
-        key, order = (cube, place) if outer else (place, cube)
+        place, plane = ((y,), (x, z)) if core == 0 else ((z,), (x, y))
+        key, order = (plane, place) if line else (place, plane)
         groups.setdefault((core, key), []).append((order, index_of(x, core, z, y)))
     return [[device for _, device in sorted(members)] for _, members in sorted(groups.items())]
 
 
-def exchange(values, outer):
-    blocks = values.reshape(8, values.shape[0] // 8, values.shape[1])
-    return lax.all_to_all(blocks, ALL, 0, 0, axis_index_groups=cube_groups(outer), tiled=True)
+def exchange(values, line):
+    groups = groups_of(line)
+    size = len(groups[0])
+    blocks = values.reshape(size, values.shape[0] // size, values.shape[1])
+    return lax.all_to_all(blocks, ALL, 0, 0, axis_index_groups=groups, tiled=True)
 
 
-def spread(values, outer):
-    copies = jnp.broadcast_to(values[None], (8,) + values.shape)
-    got = lax.all_to_all(copies, ALL, 0, 0, axis_index_groups=cube_groups(outer), tiled=True)
-    return got.reshape(8 * values.shape[0], values.shape[1])
+def spread(values, line):
+    groups = groups_of(line)
+    size = len(groups[0])
+    copies = jnp.broadcast_to(values[None], (size,) + values.shape)
+    got = lax.all_to_all(copies, ALL, 0, 0, axis_index_groups=groups, tiled=True)
+    return got.reshape(size * values.shape[0], values.shape[1])
 
 
 def added(blocks):
@@ -121,25 +123,18 @@
     far_act = jnp.maximum(dot(far, enc_2) + bias_2, 0.0)
     far_part = dot((far_act * far_act).astype(BF16), dec_2).astype(BF16)
     got_far = exchange(far_part, True)
-    core = lax.axis_index("c")
-    step = SHIFTS[0][0] + core * (SHIFTS[1][0] - SHIFTS[0][0])
-    x = 2 * lax.axis_index("xh") + lax.axis_index("xl")
-    turned = ((x + step) % 4 // 2 + step) % 2 == 1
-    low = added(got_near[:4]) + added(got_far[4:])
-    high = added(got_near[4:]) + added(got_far[:4])
-    summed = paired(turned, low, high, 1).astype(BF16)
+    rectified = paired(odd, near_act, far_act, LINE)
+    latent = (rectified * rectified).astype(BF16)
+    summed = paired(odd, added(got_near), added(got_far), 1).astype(BF16)
     misfit = (added(exchange(summed, False)) + b_dec).astype(BF16)
     misfit_all = spread(spread(misfit, False), True)
-
-    rectified = paired(odd, near_act, far_act, 8)
-    latent = (rectified * rectified).astype(BF16)
 
     own = w_dec.shape[0]
     dec_out = contract_first(latent[:, own:], misfit_all).astype(BF16)
     dec_sent = other_core(dec_out)
     misfit_all, dec_out = lax.optimization_barrier((misfit_all, dec_out))
     slope = (contract_last(misfit_all, dec_2) * 2.0 * rectified).astype(BF16)
-    slope = slope.reshape(8, 2, -1, slope.shape[1])
+    slope = slope.reshape(LINE, 2, -1, slope.shape[1])
     near_slope = jnp.where(odd, slope[:, 1], slope[:, 0]).reshape(rows, -1)
     far_slope = jnp.where(odd, slope[:, 0], slope[:, 1]).reshape(rows, -1)
     slope = jnp.concatenate([near_slope, far_slope], axis=0)

time: 154 us -> 156 us (1.013)
  starting transfers between devices: 31 us -> 15.5 us
  blocking collectives: 43 us -> 55.9 us
  other arithmetic: 7.64 us -> 9.61 us
    all_to_all x3, blocking collectives: 43 us -> 55.9 us  [the longest x2 39.2 us: exchange(): lax.all_to_all(blocks, ALL, 0, 0, axis_index_groups=groups, tiled=True)]
    all_to_all x2, starting transfers between devices: 16.8 us -> 8.34 us  [the longest x1 4.75 us: spread(): lax.all_to_all(copies, ALL, 0, 0, axis_index_groups=groups, tiled=True)]
    ppermute x5, starting transfers between devices: 10.9 us -> 3.85 us  [other_core(): return lax.ppermute(values, 'c', [(0, 1), (1, 0)])]
  transfers between devices with their start and end apart: 9 -> 9, of which waited for: 3 -> 3; matrix products, arithmetic and copies ran while one was open for 15% -> 16% of each run, Pallas kernels for 0% -> 0%
where the time goes in v1:
time: 156 us; the launch traced here: 155 us
  blocking collectives  55.9 us (36%)
  waiting for transfers between devices  40.4 us (26%)
  matrix products  25.8 us (17%)
  starting transfers between devices  15.5 us (10%)
  other arithmetic  9.61 us (6%)
  local copies, waits for them, and re-layouts  6.99 us (4%)
    all_to_all x2, blocking collectives, exchange(): lax.all_to_all(blocks, ALL, 0, 0, axis_index_groups=groups, tiled=True)  39.2 us
    all_to_all x1, waiting for transfers between devices, spread(): lax.all_to_all(copies, ALL, 0, 0, axis_index_groups=groups, tiled=True)  23.9 us
    all_to_all x1, blocking collectives, spread(): lax.all_to_all(copies, ALL, 0, 0, axis_index_groups=groups, tiled=True)  16.6 us
    dot_general x4, matrix products, contract_first(): lax.dot_general(left, right, (((0,), (0,)), ((), ())), preferred_element_...  12.5 us
    all_to_all x1, waiting for transfers between devices, exchange(): lax.all_to_all(blocks, ALL, 0, 0, axis_index_groups=groups, tiled=True)  11.8 us
    dot_general x7, matrix products, dot(): return jnp.dot(left, right, preferred_element_type=F32)  8.99 us
    all_to_all x1, starting transfers between devices, spread(): lax.all_to_all(copies, ALL, 0, 0, axis_index_groups=groups, tiled=True)  4.75 us
    ppermute x2, waiting for transfers between devices, far_rows(): return lax.ppermute(values, ALL, pairs)  4.73 us
  transfers between devices with their start and end apart: 9, of which 3 were waited for; matrix products, arithmetic and copies ran while one was open for 16% of the time, Pallas kernels for 0%

profile of v1, /device:TPU:1, one launch (start us, length us, event | category | flops | bytes accessed | tf_op | source)
XLA Modules:
  0.0 155.1 jit_solution(12991823244417862950)
XLA Ops:
  0.7 1.5 collective-permute-start.1
  2.6 2.6 %collective-permute-start = (bf16[256,3584]{1,0:T(8,128)(2,1)}, bf16[256,3584]{1,0:T(8,128)(2,1)S(1)}, u32[]{:S(2)}, u32[]{:S(2)}) collective-permute-start(bf16[256,3584]{1,0:T(8,128)(2,1)} %param.9), channel_id=1, source_target_pairs={{0,64},{1,65},{2,66},{3,67},{4,68},{5,69},{6,70},{7,71},{8,72},{9,... | collective-permute-start | bytes 5505032 | tf_op jit(solution)/shard_map/ppermute | solution.py:52
  5.2 2.0 %fusion.1 = f32[256]{0:T(256)S(1)} fusion(bf16[256,3584]{1,0:T(8,128)(2,1)} %param.9), kind=kLoop, calls=%fused_computation.7 | loop fusion | flops 2752256 | bytes 1836032 | tf_op jit(solution)/shard_map/reduce_sum | solution.py:20
  8.6 2.0 %fusion.3 = bf16[256,3584]{1,0:T(8,128)(2,1)S(1)} fusion(bf16[256,3584]{1,0:T(8,128)(2,1)} %param.9, f32[3584]{0:T(1024)S(1)} %broadcast_add_fusion.1, f32[256]{0:T(256)S(1)} %add_rsqrt_fusion), kind=kLoop, calls=%fused_computation.9 | loop fusion | flops 3670016 | bytes 3685376 | tf_op jit(solution)/shard_map/convert_element_type | solution.py:24
  11.7 1.5 copy-done.14
  18.6 2.4 %fusion = bf16[256,3584]{1,0:T(8,128)(2,1)} fusion(f32[256,3584]{1,0:T(8,128)S(1)} %fusion.31, bf16[512,3584]{1,0:T(8,128)(2,1)S(1)} %constant_dynamic-update-slice_fusion.2, f32[256,512]{1,0:T(8,128)S(1)} %fusion.9), kind=kOutput, calls=%fused_computation.1 | convolution fusion | flops 941621248 | bytes 9699328 | tf_op jit(solution)/shard_map/dot_general | solution.py:28
  21.0 4.7 %collective-permute-done = bf16[256,3584]{1,0:T(8,128)(2,1)S(1)} collective-permute-done((bf16[256,3584]{1,0:T(8,128)(2,1)}, bf16[256,3584]{1,0:T(8,128)(2,1)S(1)}, u32[]{:S(2)}, u32[]{:S(2)}) %collective-permute-start) | collective-permute-done | bytes 1835040 | tf_op jit(solution)/shard_map/ppermute | solution.py:52
  26.2 1.2 copy-done.8
  29.8 19.2 %all_to_all.25 = bf16[4,64,3584]{2,1,0:T(8,128)(2,1)} all-to-all(bf16[4,64,3584]{2,1,0:T(8,128)(2,1)S(1)} %bitcast.38), channel_id=1, replica_groups={{0,1,2,3},{4,5,6,7},{8,9,10,11},{12,13,14,15},{64,65,66,67},{68,69,70,7..., dimensions={0} | all-to-all | bytes 3670016 | tf_op jit(solution)/shard_map/all_to_all | solution.py:68
  48.9 3.6 %all-to-all-start.1 = ((bf16[4,64,3584]{2,1,0:T(8,128)(2,1)}), bf16[4,64,3584]{2,1,0:T(8,128)(2,1)S(1)}, u32[]{:S(2)}, u32[]{:S(2)}) async-start(bf16[4,64,3584]{2,1,0:T(8,128)(2,1)} %bitcast.7), calls=%async_computation.1 | async-start | bytes 3670016 | tf_op jit(solution)/shard_map/all_to_all | solution.py:68
  52.5 2.4 %add_bitcast_fusion.1 = bf16[1,1,64,3584]{3,2,1,0:T(8,128)(2,1)} fusion(bf16[4,64,3584]{2,1,0:T(8,128)(2,1)} %all_to_all.25), kind=kLoop, calls=%fused_computation.30 | loop fusion | flops 1835008 | bytes 2293760 | tf_op jit(solution)/shard_map/concatenate | solution.py:94
  55.0 11.8 %all-to-all-done.1 = bf16[4,64,3584]{2,1,0:T(8,128)(2,1)S(1)} async-done(((bf16[4,64,3584]{2,1,0:T(8,128)(2,1)}), bf16[4,64,3584]{2,1,0:T(8,128)(2,1)S(1)}, u32[]{:S(2)}, u32[]{:S(2)}) %all-to-all-start.1) | async-done | bytes 1835040 | tf_op jit(solution)/shard_map/all_to_all | solution.py:68
  67.0 1.3 fusion.5
  68.3 20.0 %all_to_all.26 = bf16[16,8,3584]{2,1,0:T(8,128)(2,1)S(1)} all-to-all(bf16[16,8,3584]{2,1,0:T(8,128)(2,1)S(1)} %bitcast.40), channel_id=1, replica_groups={{0,4,8,12,64,68,72,76,16,20,24,28,80,84,88,92},{1,5,9,13,65,69,73,77,17..., dimensions={0} | all-to-all | bytes 1835008 | tf_op jit(solution)/shard_map/all_to_all | solution.py:68
  88.5 16.6 %all_to_all.27 = bf16[16,8,3584]{2,1,0:T(8,128)(2,1)S(1)} all-to-all(bf16[16,8,3584]{2,1,0:T(8,128)(2,1)S(1)} %broadcast_in_dim.9), channel_id=1, replica_groups={{0,4,8,12,64,68,72,76,16,20,24,28,80,84,88,92},{1,5,9,13,65,69,73,77,17..., dimensions={0} | all-to-all | bytes 1835008 | tf_op jit(solution)/shard_map/all_to_all | solution.py:75
  105.2 2.1 %broadcast_in_dim.11 = bf16[4,128,3584]{2,1,0:T(8,128)(2,1)} broadcast(bf16[128,3584]{1,0:T(8,128)(2,1)S(1)} %bitcast.41), dimensions={1,2} | broadcast | bytes 4587520 | tf_op jit(solution)/shard_map/broadcast_in_dim | solution.py:74
  107.3 4.8 %all-to-all-start.4 = ((bf16[4,128,3584]{2,1,0:T(8,128)(2,1)}), bf16[4,128,3584]{2,1,0:T(8,128)(2,1)}, u32[]{:S(2)}, u32[]{:S(2)}) async-start(bf16[4,128,3584]{2,1,0:T(8,128)(2,1)} %broadcast_in_dim.11), calls=%async_computation.4 | async-start | bytes 7340032 | tf_op jit(solution)/shard_map/all_to_all | solution.py:75
  112.3 23.9 %all-to-all-done.4 = bf16[4,128,3584]{2,1,0:T(8,128)(2,1)} async-done(((bf16[4,128,3584]{2,1,0:T(8,128)(2,1)}), bf16[4,128,3584]{2,1,0:T(8,128)(2,1)}, u32[]{:S(2)}, u32[]{:S(2)}) %all-to-all-start.4) | async-done | bytes 3670048 | tf_op jit(solution)/shard_map/all_to_all | solution.py:75
  136.2 3.3 %convolution_convert_fusion.1 = bf16[256,3584]{1,0:T(8,128)(2,1)S(1)} fusion(bf16[512,3584]{1,0:T(8,128)(2,1)} %bitcast.12, bf16[512,512]{1,0:T(8,128)(2,1)S(1)} %fusion.11), kind=kOutput, calls=%fused_computation.3 | convolution fusion | flops 940441600 | bytes 5767168 | tf_op jit(solution)/shard_map/dot_general | solution.py:32
  139.5 1.8 %collective-permute-start.6 = (bf16[256,3584]{1,0:T(8,128)(2,1)S(1)}, bf16[256,3584]{1,0:T(8,128)(2,1)S(1)}, u32[]{:S(2)}, u32[]{:S(2)}) collective-permute-start(bf16[256,3584]{1,0:T(8,128)(2,1)S(1)} %convolution_convert_fusion.1), channel_id=1, source_target_pairs={{0,32},{32,0},{1,33},{33,1},{2,34},{34,2},{3,35},{35,3},{4,36},{36... | collective-permute-start | bytes 5505032 | tf_op jit(solution)/shard_map/ppermute | solution.py:87
  141.3 4.3 %fusion.7 = bf16[512,512]{1,0:T(8,128)(2,1)S(1)} fusion(f32[512,512]{1,0:T(8,128)S(1)} %bitcast.39, bf16[512,3584]{1,0:T(8,128)(2,1)} %bitcast.12, bf16[512,3584]{1,0:T(8,128)(2,1)S(1)} %copy-done.3), kind=kOutput, calls=%fused_computation.19 | convolution fusion | flops 1879834624 | bytes 8912896 | tf_op jit(solution)/shard_map/dot_general | solution.py:36
  145.6 1.2 convolution_convert_fusion
  147.0 5.0 %add_multiply_fusion = f32[256,3584]{1,0:T(8,128)} fusion(bf16[256,3584]{1,0:T(8,128)(2,1)S(1)} %collective-permute-done.6, bf16[512,3584]{1,0:T(8,128)(2,1)} %bitcast.12, bf16[512,512]{1,0:T(8,128)(2,1)S(1)} %fusion.11), kind=kOutput, calls=%fused_computation.11 | convolution fusion | flops 942276608 | bytes 9437184 | tf_op jit(solution)/shard_map/dot_general | solution.py:32
  152.0 3.0 %add_multiply_fusion.1 = f32[3584,256]{1,0:T(8,128)} fusion(bf16[3584,256]{1,0:T(8,128)(2,1)S(1)} %collective-permute-done.5, bf16[256,3584]{1,0:T(8,128)(2,1)S(1)} %copy-done.9, bf16[256,3584]{1,0:T(8,128)(2,1)S(1)} %copy-done.7, bf16[512,512]{1,0:T(8,128)(2,1)S(1)} %pad_maximum_fusion.5), kind=kOutput, calls=%fused_computation.12 | convolution fusion | flops 949616640 | bytes 9437184 | tf_op jit(solution)/shard_map/dot_general | solution.py:32
  (61 shorter events, 11.9 us)
Async XLA Ops:
  0.6 14.2 %copy-start = (bf16[448,3584]{1,0:T(8,128)(2,1)S(1)}, bf16[448,3584]{1,0:T(8,128)(2,1)}, u32[]{:S(2)}) copy-start(bf16[448,3584]{1,0:T(8,128)(2,1)} %param.13) | copy-start | bytes 9633796
  0.6 10.0 %copy-start.13 = (bf16[3584,448]{0,1:T(8,128)(2,1)S(1)}, bf16[3584,448]{0,1:T(8,128)(2,1)}, u32[]{:S(2)}) copy-start(bf16[3584,448]{0,1:T(8,128)(2,1)} %param.11) | copy-start | bytes 9633796
  0.7 16.5 %collective-permute-start.1 = (bf16[3584,256]{1,0:T(8,128)(2,1)}, bf16[3584,256]{1,0:T(8,128)(2,1)S(1)}, u32[]{:S(2)}, u32[]{:S(2)}) collective-permute-start(bf16[3584,256]{1,0:T(8,128)(2,1)} %param.14), channel_id=1, source_target_pairs={{0,32},{32,0},{1,33},{33,1},{2,34},{34,2},{3,35},{35,3},{4,36},{36... | collective-permute-start | bytes 5505032 | tf_op jit(solution)/shard_map/ppermute | solution.py:87
  2.1 15.0 %collective-permute-start.2 = (bf16[256]{0:T(256)(128)(2,1)}, bf16[256]{0:T(256)(128)(2,1)S(1)}, u32[]{:S(2)}, u32[]{:S(2)}) collective-permute-start(bf16[256]{0:T(256)(128)(2,1)} %param.15), channel_id=1, source_target_pairs={{0,32},{32,0},{1,33},{33,1},{2,34},{34,2},{3,35},{35,3},{4,36},{36... | collective-permute-start | bytes 1544 | tf_op jit(solution)/shard_map/ppermute | solution.py:87
  2.2 16.2 %collective-permute-start.3 = (bf16[256,3584]{1,0:T(8,128)(2,1)}, bf16[256,3584]{1,0:T(8,128)(2,1)S(1)}, u32[]{:S(2)}, u32[]{:S(2)}) collective-permute-start(bf16[256,3584]{1,0:T(8,128)(2,1)} %param.16), channel_id=1, source_target_pairs={{0,32},{32,0},{1,33},{33,1},{2,34},{34,2},{3,35},{35,3},{4,36},{36... | collective-permute-start | bytes 5505032 | tf_op jit(solution)/shard_map/ppermute | solution.py:87
  2.6 23.1 %collective-permute-start = (bf16[256,3584]{1,0:T(8,128)(2,1)}, bf16[256,3584]{1,0:T(8,128)(2,1)S(1)}, u32[]{:S(2)}, u32[]{:S(2)}) collective-permute-start(bf16[256,3584]{1,0:T(8,128)(2,1)} %param.9), channel_id=1, source_target_pairs={{0,64},{1,65},{2,66},{3,67},{4,68},{5,69},{6,70},{7,71},{8,72},{9,... | collective-permute-start | bytes 5505032 | tf_op jit(solution)/shard_map/ppermute | solution.py:52
  7.2 18.5 %collective-permute-start.4 = (f32[256,1]{0,1:T(1,128)S(1)}, f32[256,1]{0,1:T(1,128)S(1)}, u32[]{:S(2)}, u32[]{:S(2)}) collective-permute-start(f32[256,1]{0,1:T(1,128)S(1)} %bitcast.49), channel_id=1, source_target_pairs={{0,64},{1,65},{2,66},{3,67},{4,68},{5,69},{6,70},{7,71},{8,72},{9,... | collective-permute-start | bytes 3080 | tf_op jit(solution)/shard_map/ppermute | solution.py:52
  10.6 6.7 %copy-start.6 = (bf16[256,3584]{1,0:T(8,128)(2,1)}, bf16[256,3584]{1,0:T(8,128)(2,1)S(1)}, u32[]{:S(2)}) copy-start(bf16[256,3584]{1,0:T(8,128)(2,1)S(1)} %fusion.3) | copy-start | bytes 5505028
  10.6 2.6 %copy-start.14 = (bf16[3584,448]{0,1:T(8,128)(2,1)S(1)}, bf16[3584,448]{0,1:T(8,128)(2,1)}, u32[]{:S(2)}) copy-start(bf16[3584,448]{0,1:T(8,128)(2,1)} %param.12) | copy-start | bytes 9633796
  13.2 1.5 copy-start.4
  14.9 1.5 copy-start.5
  16.4 0.7 copy-start.10
  16.4 0.7 copy-start.12
  18.5 10.1 %copy-start.2 = (bf16[512,3584]{1,0:T(8,128)(2,1)}, bf16[512,3584]{1,0:T(8,128)(2,1)S(1)}, u32[]{:S(2)}) copy-start(bf16[512,3584]{1,0:T(8,128)(2,1)S(1)} %constant_dynamic-update-slice_fusion.2) | copy-start | bytes 11010052
  26.2 1.2 copy-start.8
  48.9 17.8 %all-to-all-start.1 = ((bf16[4,64,3584]{2,1,0:T(8,128)(2,1)}), bf16[4,64,3584]{2,1,0:T(8,128)(2,1)S(1)}, u32[]{:S(2)}, u32[]{:S(2)}) async-start(bf16[4,64,3584]{2,1,0:T(8,128)(2,1)} %bitcast.7), calls=%async_computation.1 | async-start | bytes 3670016 | tf_op jit(solution)/shard_map/all_to_all | solution.py:68
  52.5 35.8 %copy-start.11 = (f32[3584]{0:T(1024)S(1)}, f32[3584]{0:T(1024)}, u32[]{:S(2)}) copy-start(f32[3584]{0:T(1024)} %param.17) | copy-start | bytes 43012
  107.3 28.9 %all-to-all-start.4 = ((bf16[4,128,3584]{2,1,0:T(8,128)(2,1)}), bf16[4,128,3584]{2,1,0:T(8,128)(2,1)}, u32[]{:S(2)}, u32[]{:S(2)}) async-start(bf16[4,128,3584]{2,1,0:T(8,128)(2,1)} %broadcast_in_dim.11), calls=%async_computation.4 | async-start | bytes 7340032 | tf_op jit(solution)/shard_map/all_to_all | solution.py:75
  136.2 5.1 %copy-start.3 = (bf16[512,3584]{1,0:T(8,128)(2,1)S(1)}, bf16[512,3584]{1,0:T(8,128)(2,1)}, u32[]{:S(2)}) copy-start(bf16[512,3584]{1,0:T(8,128)(2,1)} %copy-done.2) | copy-start | bytes 11010052
  139.5 7.5 %collective-permute-start.6 = (bf16[256,3584]{1,0:T(8,128)(2,1)S(1)}, bf16[256,3584]{1,0:T(8,128)(2,1)S(1)}, u32[]{:S(2)}, u32[]{:S(2)}) collective-permute-start(bf16[256,3584]{1,0:T(8,128)(2,1)S(1)} %convolution_convert_fusion.1), channel_id=1, source_target_pairs={{0,32},{32,0},{1,33},{33,1},{2,34},{34,2},{3,35},{35,3},{4,36},{36... | collective-permute-start | bytes 5505032 | tf_op jit(solution)/shard_map/ppermute | solution.py:87
  141.3 4.3 %copy-start.7 = (bf16[256,3584]{1,0:T(8,128)(2,1)S(1)}, bf16[256,3584]{1,0:T(8,128)(2,1)}, u32[]{:S(2)}) copy-start(bf16[256,3584]{1,0:T(8,128)(2,1)} %copy-done.6) | copy-start | bytes 5505028
  141.3 4.3 %copy-start.9 = (bf16[256,3584]{1,0:T(8,128)(2,1)S(1)}, bf16[256,3584]{1,0:T(8,128)(2,1)}, u32[]{:S(2)}) copy-start(bf16[256,3584]{1,0:T(8,128)(2,1)} %copy-done.8) | copy-start | bytes 5505028
  146.8 5.2 %collective-permute-start.5 = (bf16[3584,256]{1,0:T(8,128)(2,1)S(1)}, bf16[3584,256]{1,0:T(8,128)(2,1)S(1)}, u32[]{:S(2)}, u32[]{:S(2)}) collective-permute-start(bf16[3584,256]{1,0:T(8,128)(2,1)S(1)} %convolution_convert_fusion), channel_id=1, source_target_pairs={{0,32},{32,0},{1,33},{33,1},{2,34},{34,2},{3,35},{35,3},{4,36},{36... | collective-permute-start | bytes 5505032 | tf_op jit(solution)/shard_map/ppermute | solution.py:87
  152.0 3.0 %copy-start.1 = (bf16[448,3584]{1,0:T(8,128)(2,1)S(1)}, bf16[448,3584]{1,0:T(8,128)(2,1)}, u32[]{:S(2)}) copy-start(bf16[448,3584]{1,0:T(8,128)(2,1)} %param.13) | copy-start | bytes 9633796
